TPU v7x, 32 devices: a whole 2x2x4 slice. The times are simulated.
32 devices in a mesh: tile: 16 (over z, x, core), mem: 2 (over y).
Axes of the slice: x: 2, y: 2, z: 4, core: 2. Of those that a mesh axis runs over, the one named last changes fastest.
Arguments:
- ensemble: float32 [64, 7, 32768], P('mem', None, 'tile'), may hold values from -6 to 6
- obs_site: int32 [8, 32], replicated, may hold values from 0 to 14335
- obs_value: float32 [8, 32], replicated, may hold values from -8 to 8
- obs_var: float32 [8, 32], replicated, may hold values from 4 to 32
- owner_tile: int32 [8], replicated, may hold values from 0 to 15
- tile_mask: int32 [8, 16], replicated, may hold values 0 or 1
- batch_order: int32 [8], replicated, may hold values from 0 to 7, each once
Outputs:
- posterior: float32 [64, 7, 32768], P('mem', None, 'tile')
All inputs are finite; a program needn't handle non-finite values.
Results may differ from a plain program's by a relative error of at most 0.0001.
Values sent between devices are 32-bit elements; how exact they have to be, the bound alone decides.
No kernel may reach another device: no remote copies, remote signals or barrier semaphores. Data moves between devices by JAX's collectives and lax.ppermute only.
A program may use at most 64 MiB of HBM per device.

v0:
```python
import jax
import jax.numpy as jnp
from jax import lax
from jax.sharding import PartitionSpec as P

BATCHES = 8


def from_root(block, axis, holder):
    block = jnp.where(lax.axis_index(axis) == holder, block, jnp.zeros_like(block))
    return lax.psum(block, axis)


def batch_transform(priors, values, variances):
    count = priors.shape[1]
    highest = lax.Precision.HIGHEST

    def assimilate(transform, inputs):
        prior_row, value, variance = inputs
        y_row = jnp.dot(prior_row, transform, precision=highest)
        ens_mean = jnp.mean(y_row)
        spread = y_row - ens_mean
        sample_var = jnp.sum(spread * spread) / (count - 1)
        inv_total = 1.0 / (sample_var + variance)
        alpha = 1.0 / (1.0 + jnp.sqrt(variance * inv_total))
        weights = inv_total / (count - 1) * (value - ens_mean - alpha * spread)
        moved = jnp.dot(transform, spread, precision=highest)
        return (transform + moved[:, None] * weights[None, :], None)

    start_eye = jnp.eye(count, dtype=jnp.float32)
    result, _ = lax.scan(assimilate, start_eye, (priors, values, variances))
    return result


def body(ensemble, obs_site, obs_value, obs_var, owner_tile, tile_mask, batch_order):
    highest = lax.Precision.HIGHEST
    local_members = ensemble.shape[0]
    all_members = local_members * lax.axis_size("mem")
    tile_idx = lax.axis_index("tile")
    mem_idx = lax.axis_index("mem")
    flat_state = ensemble.reshape(local_members, -1)
    combined = jnp.eye(all_members, dtype=jnp.float32)
    for position in range(BATCHES):
        batch_id = batch_order[position]
        local_rows = jnp.take(flat_state, obs_site[batch_id], axis=1)
        obs_rows = lax.all_gather(local_rows, "mem", axis=0, tiled=True)
        own_priors = jnp.dot(obs_rows.T, combined, precision=highest)
        priors = from_root(own_priors, "tile", owner_tile[batch_id])
        transform = batch_transform(priors, obs_value[batch_id], obs_var[batch_id])
        updated = jnp.dot(combined, transform, precision=highest)
        combined = jnp.where(
            (tile_mask[batch_id, tile_idx] == 1) | (owner_tile[batch_id] == tile_idx),
            updated,
            combined,
        )
    my_columns = lax.dynamic_slice_in_dim(combined, mem_idx * local_members, local_members, 1)
    return jnp.einsum(
        "mn,mvc->nvc",
        my_columns,
        lax.all_gather(ensemble, "mem", axis=0, tiled=True),
        precision=highest,
    )


def solution(mesh):
    return jax.shard_map(
        body,
        mesh=mesh,
        in_specs=(P("mem", None, "tile"), P(), P(), P(), P(), P(), P()),
        out_specs=P("mem", None, "tile"),
        check_vma=False,
    )
```

profile of v0, /device:TPU:0, one launch (start us, length us, event | category | flops | bytes accessed | tf_op | source)
XLA Modules:
  0.0 2158.5 jit_solution(17621511112711468717)
XLA Ops:
  18.7 6.0 copy.17
  43.0 5.8 all_gather.27
  49.0 61.2 %psum.56 = f32[32,64]{1,0:T(8,128)S(1)} all-reduce(f32[32,64]{1,0:T(8,128)S(1)} %convolution_select_fusion.14), channel_id=1, replica_groups=mesh['tile'=16,'mem'=2] {'tile'}, use_global_device_ids=true, to_apply=%region_0.0 | all-reduce | flops 2048 | bytes 16384 | tf_op jit(solution)/shard_map/psum | solution.py:11
  110.2 211.1 %while.80 = (s32[]{:T(128)}, f32[64,64]{1,0:T(8,128)S(1)}, f32[32,64]{1,0:T(8,128)S(1)}, f32[32]{0:T(128)S(1)}, f32[32]{0:T(128)S(1)}, /*index=5*/s32[]{:T(128)}, f32[]{:T(128)}, f32[]{:T(128)}, f32[]{:T(128)}) while((s32[]{:T(128)}, f32[64,64]{1,0:T(8,128)S(1)}, f32[32,64]{1,0:T(8,128)S(1)}, f32[32]{0:T(128)S(1)}, f32[32]{0:T(128)S(1)}, ...), condition=%wide.region_4.6_spmd, body=%wide.region_1.0_spmd.sunk | while | flops 107081 | bytes 84749 | solution.py:31
  325.2 4.4 all_gather.28
  331.3 57.6 %psum.57 = f32[32,64]{1,0:T(8,128)S(1)} all-reduce(f32[32,64]{1,0:T(8,128)S(1)} %convolution_select_fusion.13), channel_id=1, replica_groups=mesh['tile'=16,'mem'=2] {'tile'}, use_global_device_ids=true, to_apply=%region_5.7 | all-reduce | flops 2048 | bytes 16384 | tf_op jit(solution)/shard_map/psum | solution.py:11
  388.9 195.8 %while.81 = (s32[]{:T(128)}, f32[64,64]{1,0:T(8,128)S(1)}, f32[32,64]{1,0:T(8,128)S(1)}, f32[32]{0:T(128)S(1)}, f32[32]{0:T(128)S(1)}, /*index=5*/s32[]{:T(128)}, f32[]{:T(128)}, f32[]{:T(128)}, f32[]{:T(128)}) while((s32[]{:T(128)}, f32[64,64]{1,0:T(8,128)S(1)}, f32[32,64]{1,0:T(8,128)S(1)}, f32[32]{0:T(128)S(1)}, f32[32]{0:T(128)S(1)}, ...), condition=%wide.region_9.11_spmd, body=%wide.region_6.10_spmd.sunk | while | flops 107081 | bytes 84749 | solution.py:31
  589.2 4.4 all_gather.29
  594.1 57.6 %psum.58 = f32[32,64]{1,0:T(8,128)S(1)} all-reduce(f32[32,64]{1,0:T(8,128)S(1)} %convolution_select_fusion.12), channel_id=1, replica_groups=mesh['tile'=16,'mem'=2] {'tile'}, use_global_device_ids=true, to_apply=%region_10.12 | all-reduce | flops 2048 | bytes 16384 | tf_op jit(solution)/shard_map/psum | solution.py:11
  651.7 183.3 %while.82 = (s32[]{:T(128)}, f32[64,64]{1,0:T(8,128)S(1)}, f32[32,64]{1,0:T(8,128)S(1)}, f32[32]{0:T(128)S(1)}, f32[32]{0:T(128)S(1)}, /*index=5*/s32[]{:T(128)}, f32[]{:T(128)}, f32[]{:T(128)}, f32[]{:T(128)}) while((s32[]{:T(128)}, f32[64,64]{1,0:T(8,128)S(1)}, f32[32,64]{1,0:T(8,128)S(1)}, f32[32]{0:T(128)S(1)}, f32[32]{0:T(128)S(1)}, ...), condition=%wide.region_14.16_spmd, body=%wide.region_11.15_spmd.sunk | while | flops 107081 | bytes 84749 | solution.py:31
  839.5 4.4 all_gather.30
  844.4 57.6 %psum.59 = f32[32,64]{1,0:T(8,128)S(1)} all-reduce(f32[32,64]{1,0:T(8,128)S(1)} %convolution_select_fusion.11), channel_id=1, replica_groups=mesh['tile'=16,'mem'=2] {'tile'}, use_global_device_ids=true, to_apply=%region_15.17 | all-reduce | flops 2048 | bytes 16384 | tf_op jit(solution)/shard_map/psum | solution.py:11
  902.0 185.8 %while.83 = (s32[]{:T(128)}, f32[64,64]{1,0:T(8,128)S(1)}, f32[32,64]{1,0:T(8,128)S(1)}, f32[32]{0:T(128)S(1)}, f32[32]{0:T(128)S(1)}, /*index=5*/s32[]{:T(128)}, f32[]{:T(128)}, f32[]{:T(128)}, f32[]{:T(128)}) while((s32[]{:T(128)}, f32[64,64]{1,0:T(8,128)S(1)}, f32[32,64]{1,0:T(8,128)S(1)}, f32[32]{0:T(128)S(1)}, f32[32]{0:T(128)S(1)}, ...), condition=%wide.region_19.21_spmd, body=%wide.region_16.20_spmd.sunk | while | flops 107081 | bytes 84749 | solution.py:31
  1097.2 57.6 %psum.60 = f32[32,64]{1,0:T(8,128)S(1)} all-reduce(f32[32,64]{1,0:T(8,128)S(1)} %convolution_select_fusion.10), channel_id=1, replica_groups=mesh['tile'=16,'mem'=2] {'tile'}, use_global_device_ids=true, to_apply=%region_20.22 | all-reduce | flops 2048 | bytes 16384 | tf_op jit(solution)/shard_map/psum | solution.py:11
  1154.8 194.4 %while.84 = (s32[]{:T(128)}, f32[64,64]{1,0:T(8,128)S(1)}, f32[32,64]{1,0:T(8,128)S(1)}, f32[32]{0:T(128)S(1)}, f32[32]{0:T(128)S(1)}, /*index=5*/s32[]{:T(128)}, f32[]{:T(128)}, f32[]{:T(128)}, f32[]{:T(128)}) while((s32[]{:T(128)}, f32[64,64]{1,0:T(8,128)S(1)}, f32[32,64]{1,0:T(8,128)S(1)}, f32[32]{0:T(128)S(1)}, f32[32]{0:T(128)S(1)}, ...), condition=%wide.region_24.26_spmd, body=%wide.region_21.25_spmd.sunk | while | flops 107081 | bytes 84749 | solution.py:31
  1353.7 4.4 all_gather.32
  1358.6 57.6 %psum.61 = f32[32,64]{1,0:T(8,128)S(1)} all-reduce(f32[32,64]{1,0:T(8,128)S(1)} %convolution_select_fusion.9), channel_id=1, replica_groups=mesh['tile'=16,'mem'=2] {'tile'}, use_global_device_ids=true, to_apply=%region_25.27 | all-reduce | flops 2048 | bytes 16384 | tf_op jit(solution)/shard_map/psum | solution.py:11
  1416.2 184.1 %while.85 = (s32[]{:T(128)}, f32[64,64]{1,0:T(8,128)S(1)}, f32[32,64]{1,0:T(8,128)S(1)}, f32[32]{0:T(128)S(1)}, f32[32]{0:T(128)S(1)}, /*index=5*/s32[]{:T(128)}, f32[]{:T(128)}, f32[]{:T(128)}, f32[]{:T(128)}) while((s32[]{:T(128)}, f32[64,64]{1,0:T(8,128)S(1)}, f32[32,64]{1,0:T(8,128)S(1)}, f32[32]{0:T(128)S(1)}, f32[32]{0:T(128)S(1)}, ...), condition=%wide.region_29.31_spmd, body=%wide.region_26.30_spmd.sunk | while | flops 107081 | bytes 84749 | solution.py:31
  1604.8 4.4 all_gather.33
  1609.6 57.6 %psum.62 = f32[32,64]{1,0:T(8,128)S(1)} all-reduce(f32[32,64]{1,0:T(8,128)S(1)} %convolution_select_fusion.8), channel_id=1, replica_groups=mesh['tile'=16,'mem'=2] {'tile'}, use_global_device_ids=true, to_apply=%region_30.32 | all-reduce | flops 2048 | bytes 16384 | tf_op jit(solution)/shard_map/psum | solution.py:11
  1667.3 195.4 %while.86 = (s32[]{:T(128)}, f32[64,64]{1,0:T(8,128)S(1)}, f32[32,64]{1,0:T(8,128)S(1)}, f32[32]{0:T(128)S(1)}, f32[32]{0:T(128)S(1)}, /*index=5*/s32[]{:T(128)}, f32[]{:T(128)}, f32[]{:T(128)}, f32[]{:T(128)}) while((s32[]{:T(128)}, f32[64,64]{1,0:T(8,128)S(1)}, f32[32,64]{1,0:T(8,128)S(1)}, f32[32]{0:T(128)S(1)}, f32[32]{0:T(128)S(1)}, ...), condition=%wide.region_34.36_spmd, body=%wide.region_31.35_spmd.sunk | while | flops 107081 | bytes 84749 | solution.py:31
  1872.7 57.6 %psum.63 = f32[32,64]{1,0:T(8,128)S(1)} all-reduce(f32[32,64]{1,0:T(8,128)S(1)} %convolution_select_fusion.7), channel_id=1, replica_groups=mesh['tile'=16,'mem'=2] {'tile'}, use_global_device_ids=true, to_apply=%region_35.37 | all-reduce | flops 2048 | bytes 16384 | tf_op jit(solution)/shard_map/psum | solution.py:11
  1930.3 214.7 %while.87 = (s32[]{:T(128)}, f32[64,64]{1,0:T(8,128)S(1)}, f32[32,64]{1,0:T(8,128)S(1)}, f32[32]{0:T(128)S(1)}, f32[32]{0:T(128)S(1)}, /*index=5*/s32[]{:T(128)}, f32[]{:T(128)}, f32[]{:T(128)}, f32[]{:T(128)}) while((s32[]{:T(128)}, f32[64,64]{1,0:T(8,128)S(1)}, f32[32,64]{1,0:T(8,128)S(1)}, f32[32]{0:T(128)S(1)}, f32[32]{0:T(128)S(1)}, ...), condition=%wide.region_39.41_spmd, body=%wide.region_36.40_spmd.sunk | while | flops 107081 | bytes 84749 | solution.py:31
  2146.5 5.1 fusion.34
  (1869 shorter events, 789.0 us)
Async XLA Ops:
  6.5 23.1 %copy-start = (s32[8]{0:T(128)S(1)}, s32[8]{0:T(128)}, u32[]{:S(2)}) copy-start(s32[8]{0:T(128)} %param.29) | copy-start | bytes 100
  6.5 32.6 %copy-start.4 = (s32[8,32]{1,0:T(8,128)S(1)}, s32[8,32]{1,0:T(8,128)}, u32[]{:S(2)}) copy-start(s32[8,32]{1,0:T(8,128)} %param.26) | copy-start | bytes 3076
  6.5 103.7 %copy-start.2 = (f32[8,32]{1,0:T(8,128)S(1)}, f32[8,32]{1,0:T(8,128)}, u32[]{:S(2)}) copy-start(f32[8,32]{1,0:T(8,128)} %param.27) | copy-start | bytes 3076
  6.5 103.7 %copy-start.1 = (f32[8,32]{1,0:T(8,128)S(1)}, f32[8,32]{1,0:T(8,128)}, u32[]{:S(2)}) copy-start(f32[8,32]{1,0:T(8,128)} %param.28) | copy-start | bytes 3076
  6.5 323.0 %copy-start.3 = (s32[8,16]{1,0:T(8,128)S(1)}, s32[8,16]{1,0:T(8,128)}, u32[]{:S(2)}) copy-start(s32[8,16]{1,0:T(8,128)} %param.30) | copy-start | bytes 1540
  6.5 2140.0 %all-gather.2.cloned.1.call-start = ((), (), s32[]{:S(2)}) async-start(), calls=%async_computation | async-start | bytes 5505024 | tf_op jit(solution)/shard_map/all_gather | solution.py:60
Sparse Core Ops, SparseCore 0:
  8.9 53.8 all-gather.1
where the time goes:
time: 2170 us; the launch traced here: 2160 us
  loops' own time  822 us (38%)
  blocking collectives  501 us (23%)
  local copies, waits for them, and re-layouts  355 us (16%)
  matrix products  251 us (12%)
  other arithmetic  184 us (8%)
  between operations  43.6 us (2%)
    another operation x8, loops' own time, batch_transform(): result, _ = lax.scan(assimilate, start_eye, (priors, values, variances))  822 us
    psum x8, blocking collectives, from_root(): return lax.psum(block, axis)  465 us
    dynamic_slice x512, local copies, waits for them, and re-layouts, batch_transform(): result, _ = lax.scan(assimilate, start_eye, (priors, values, variances))  316 us
    dot_general x256, matrix products, assimilate(): y_row = jnp.dot(prior_row, transform, precision=highest)  207 us
    reduce_sum x256, other arithmetic, assimilate(): sample_var = jnp.sum(spread * spread) / (count - 1)  161 us
  transfers between devices with their start and end apart: 1, of which 0 were waited for; matrix products, arithmetic and copies ran while one was open for 36% of the time, Pallas kernels for 0%

commit v1 on v0

--- a/solution.py
+++ b/solution.py
@@ -6,9 +6,13 @@
 BATCHES = 8
 
 
+def meshes_draft(xs, axis_key):
+    return jax.lax.all_gather(xs, axis_key).sum(axis=0)
+
+
 def from_root(block, axis, holder):
     block = jnp.where(lax.axis_index(axis) == holder, block, jnp.zeros_like(block))
-    return lax.psum(block, axis)
+    return meshes_draft(block, axis)
 
 
 def batch_transform(priors, values, variances):

time: 2170 us -> 1860 us (0.86)
  blocking collectives: 501 us -> 191 us
    psum x8 -> x0, blocking collectives: 465 us -> none  [from_root(): return lax.psum(block, axis)]
    all_gather x0 -> x8, blocking collectives: none -> 154 us  [meshes_draft(): return jax.lax.all_gather(xs, axis_key).sum(axis=0)]
  transfers between devices with their start and end apart: 1 -> 1, of which waited for: 0 -> 0; matrix products, arithmetic and copies ran while one was open for 36% -> 43% of each run, Pallas kernels for 0% -> 0%
where the time goes in v1:
time: 1860 us; the launch traced here: 1850 us
  loops' own time  822 us (44%)
  local copies, waits for them, and re-layouts  355 us (19%)
  matrix products  252 us (14%)
  blocking collectives  191 us (10%)
  other arithmetic  184 us (10%)
  between operations  43.6 us (2%)
    another operation x8, loops' own time, batch_transform(): result, _ = lax.scan(assimilate, start_eye, (priors, values, variances))  822 us
    dynamic_slice x512, local copies, waits for them, and re-layouts, batch_transform(): result, _ = lax.scan(assimilate, start_eye, (priors, values, variances))  316 us
    dot_general x256, matrix products, assimilate(): y_row = jnp.dot(prior_row, transform, precision=highest)  207 us
    reduce_sum x256, other arithmetic, assimilate(): sample_var = jnp.sum(spread * spread) / (count - 1)  161 us
    all_gather x8, blocking collectives, meshes_draft(): return jax.lax.all_gather(xs, axis_key).sum(axis=0)  154 us
  transfers between devices with their start and end apart: 1, of which 0 were waited for; matrix products, arithmetic and copies ran while one was open for 43% of the time, Pallas kernels for 0%

profile of v1, /device:TPU:0, one launch (start us, length us, event | category | flops | bytes accessed | tf_op | source)
XLA Modules:
  0.0 1848.3 jit_solution(6882481702128962476)
XLA Ops:
  18.7 6.0 copy.17
  43.0 5.8 all_gather.75
  49.0 22.9 %all-gather = f32[512,64]{1,0:T(8,128)S(1)} all-gather(f32[32,64]{1,0:T(8,128)S(1)} %convolution_select_fusion.14), channel_id=2, replica_groups=mesh['tile'=16,'mem'=2] {'tile'}, dimensions={0}, use_global_device_ids=true | all-gather | bytes 139264 | tf_op jit(solution)/shard_map/all_gather | solution.py:10
  71.9 211.1 %while.80 = (s32[]{:T(128)}, f32[64,64]{1,0:T(8,128)S(1)}, f32[32,64]{1,0:T(8,128)S(1)}, f32[32]{0:T(128)S(1)}, f32[32]{0:T(128)S(1)}, /*index=5*/s32[]{:T(128)}, f32[]{:T(128)}, f32[]{:T(128)}, f32[]{:T(128)}) while((s32[]{:T(128)}, f32[64,64]{1,0:T(8,128)S(1)}, f32[32,64]{1,0:T(8,128)S(1)}, f32[32]{0:T(128)S(1)}, f32[32]{0:T(128)S(1)}, ...), condition=%wide.region_4.6_spmd, body=%wide.region_1.0_spmd.sunk | while | flops 107081 | bytes 84749 | solution.py:35
  286.8 4.4 all_gather.78
  293.0 17.8 all-gather.1
  310.8 195.8 %while.81 = (s32[]{:T(128)}, f32[64,64]{1,0:T(8,128)S(1)}, f32[32,64]{1,0:T(8,128)S(1)}, f32[32]{0:T(128)S(1)}, f32[32]{0:T(128)S(1)}, /*index=5*/s32[]{:T(128)}, f32[]{:T(128)}, f32[]{:T(128)}, f32[]{:T(128)}) while((s32[]{:T(128)}, f32[64,64]{1,0:T(8,128)S(1)}, f32[32,64]{1,0:T(8,128)S(1)}, f32[32]{0:T(128)S(1)}, f32[32]{0:T(128)S(1)}, ...), condition=%wide.region_9.11_spmd, body=%wide.region_6.10_spmd.sunk | while | flops 107081 | bytes 84749 | solution.py:35
  511.2 4.4 all_gather.81
  516.0 19.9 %all-gather.2 = f32[512,64]{1,0:T(8,128)S(1)} all-gather(f32[32,64]{1,0:T(8,128)S(1)} %convolution_select_fusion.12), channel_id=4, replica_groups=mesh['tile'=16,'mem'=2] {'tile'}, dimensions={0}, use_global_device_ids=true | all-gather | bytes 139264 | tf_op jit(solution)/shard_map/all_gather | solution.py:10
  536.0 183.3 %while.82 = (s32[]{:T(128)}, f32[64,64]{1,0:T(8,128)S(1)}, f32[32,64]{1,0:T(8,128)S(1)}, f32[32]{0:T(128)S(1)}, f32[32]{0:T(128)S(1)}, /*index=5*/s32[]{:T(128)}, f32[]{:T(128)}, f32[]{:T(128)}, f32[]{:T(128)}) while((s32[]{:T(128)}, f32[64,64]{1,0:T(8,128)S(1)}, f32[32,64]{1,0:T(8,128)S(1)}, f32[32]{0:T(128)S(1)}, f32[32]{0:T(128)S(1)}, ...), condition=%wide.region_14.16_spmd, body=%wide.region_11.15_spmd.sunk | while | flops 107081 | bytes 84749 | solution.py:35
  723.8 4.4 all_gather.84
  728.7 17.8 all-gather.3
  746.6 185.8 %while.83 = (s32[]{:T(128)}, f32[64,64]{1,0:T(8,128)S(1)}, f32[32,64]{1,0:T(8,128)S(1)}, f32[32]{0:T(128)S(1)}, f32[32]{0:T(128)S(1)}, /*index=5*/s32[]{:T(128)}, f32[]{:T(128)}, f32[]{:T(128)}, f32[]{:T(128)}) while((s32[]{:T(128)}, f32[64,64]{1,0:T(8,128)S(1)}, f32[32,64]{1,0:T(8,128)S(1)}, f32[32]{0:T(128)S(1)}, f32[32]{0:T(128)S(1)}, ...), condition=%wide.region_19.21_spmd, body=%wide.region_16.20_spmd.sunk | while | flops 107081 | bytes 84749 | solution.py:35
  936.9 4.4 all_gather.87
  941.8 19.9 %all-gather.4 = f32[512,64]{1,0:T(8,128)S(1)} all-gather(f32[32,64]{1,0:T(8,128)S(1)} %convolution_select_fusion.10), channel_id=6, replica_groups=mesh['tile'=16,'mem'=2] {'tile'}, dimensions={0}, use_global_device_ids=true | all-gather | bytes 139264 | tf_op jit(solution)/shard_map/all_gather | solution.py:10
  961.7 194.4 %while.84 = (s32[]{:T(128)}, f32[64,64]{1,0:T(8,128)S(1)}, f32[32,64]{1,0:T(8,128)S(1)}, f32[32]{0:T(128)S(1)}, f32[32]{0:T(128)S(1)}, /*index=5*/s32[]{:T(128)}, f32[]{:T(128)}, f32[]{:T(128)}, f32[]{:T(128)}) while((s32[]{:T(128)}, f32[64,64]{1,0:T(8,128)S(1)}, f32[32,64]{1,0:T(8,128)S(1)}, f32[32]{0:T(128)S(1)}, f32[32]{0:T(128)S(1)}, ...), condition=%wide.region_24.26_spmd, body=%wide.region_21.25_spmd.sunk | while | flops 107081 | bytes 84749 | solution.py:35
  1160.6 4.4 all_gather.90
  1165.5 17.8 all-gather.5
  1183.4 184.1 %while.85 = (s32[]{:T(128)}, f32[64,64]{1,0:T(8,128)S(1)}, f32[32,64]{1,0:T(8,128)S(1)}, f32[32]{0:T(128)S(1)}, f32[32]{0:T(128)S(1)}, /*index=5*/s32[]{:T(128)}, f32[]{:T(128)}, f32[]{:T(128)}, f32[]{:T(128)}) while((s32[]{:T(128)}, f32[64,64]{1,0:T(8,128)S(1)}, f32[32,64]{1,0:T(8,128)S(1)}, f32[32]{0:T(128)S(1)}, f32[32]{0:T(128)S(1)}, ...), condition=%wide.region_29.31_spmd, body=%wide.region_26.30_spmd.sunk | while | flops 107081 | bytes 84749 | solution.py:35
  1376.8 19.9 %all-gather.6 = f32[512,64]{1,0:T(8,128)S(1)} all-gather(f32[32,64]{1,0:T(8,128)S(1)} %convolution_select_fusion.8), channel_id=8, replica_groups=mesh['tile'=16,'mem'=2] {'tile'}, dimensions={0}, use_global_device_ids=true | all-gather | bytes 139264 | tf_op jit(solution)/shard_map/all_gather | solution.py:10
  1396.8 195.5 %while.86 = (s32[]{:T(128)}, f32[64,64]{1,0:T(8,128)S(1)}, f32[32,64]{1,0:T(8,128)S(1)}, f32[32]{0:T(128)S(1)}, f32[32]{0:T(128)S(1)}, /*index=5*/s32[]{:T(128)}, f32[]{:T(128)}, f32[]{:T(128)}, f32[]{:T(128)}) while((s32[]{:T(128)}, f32[64,64]{1,0:T(8,128)S(1)}, f32[32,64]{1,0:T(8,128)S(1)}, f32[32]{0:T(128)S(1)}, f32[32]{0:T(128)S(1)}, ...), condition=%wide.region_34.36_spmd, body=%wide.region_31.35_spmd.sunk | while | flops 107081 | bytes 84749 | solution.py:35
  1602.2 17.8 all-gather.7
  1620.1 214.7 %while.87 = (s32[]{:T(128)}, f32[64,64]{1,0:T(8,128)S(1)}, f32[32,64]{1,0:T(8,128)S(1)}, f32[32]{0:T(128)S(1)}, f32[32]{0:T(128)S(1)}, /*index=5*/s32[]{:T(128)}, f32[]{:T(128)}, f32[]{:T(128)}, f32[]{:T(128)}) while((s32[]{:T(128)}, f32[64,64]{1,0:T(8,128)S(1)}, f32[32,64]{1,0:T(8,128)S(1)}, f32[32]{0:T(128)S(1)}, f32[32]{0:T(128)S(1)}, ...), condition=%wide.region_39.41_spmd, body=%wide.region_36.40_spmd.sunk | while | flops 107081 | bytes 84749 | solution.py:35
  1836.3 5.1 fusion.34
  (1877 shorter events, 789.3 us)
Async XLA Ops:
  6.5 23.1 %copy-start = (s32[8]{0:T(128)S(1)}, s32[8]{0:T(128)}, u32[]{:S(2)}) copy-start(s32[8]{0:T(128)} %param.29) | copy-start | bytes 100
  6.5 32.6 %copy-start.4 = (s32[8,32]{1,0:T(8,128)S(1)}, s32[8,32]{1,0:T(8,128)}, u32[]{:S(2)}) copy-start(s32[8,32]{1,0:T(8,128)} %param.26) | copy-start | bytes 3076
  6.5 65.3 %copy-start.2 = (f32[8,32]{1,0:T(8,128)S(1)}, f32[8,32]{1,0:T(8,128)}, u32[]{:S(2)}) copy-start(f32[8,32]{1,0:T(8,128)} %param.27) | copy-start | bytes 3076
  6.5 65.4 %copy-start.1 = (f32[8,32]{1,0:T(8,128)S(1)}, f32[8,32]{1,0:T(8,128)}, u32[]{:S(2)}) copy-start(f32[8,32]{1,0:T(8,128)} %param.28) | copy-start | bytes 3076
  6.5 284.7 %copy-start.3 = (s32[8,16]{1,0:T(8,128)S(1)}, s32[8,16]{1,0:T(8,128)}, u32[]{:S(2)}) copy-start(s32[8,16]{1,0:T(8,128)} %param.30) | copy-start | bytes 1540
  6.5 1829.8 %all-gather.10.cloned.1.call-start = ((), (), s32[]{:S(2)}) async-start(), calls=%async_computation | async-start | bytes 5505024 | tf_op jit(solution)/shard_map/all_gather | solution.py:64
Sparse Core Ops, SparseCore 0:
  8.9 53.8 all-gather.9
